TPU v7x, 32 devices: a whole 2x2x4 slice. The times are simulated.
32 devices in a mesh: branch: 2 (over x), sample: 16 (over z, y, core).
Axes of the slice: x: 2, y: 2, z: 4, core: 2. Of those that a mesh axis runs over, the one named last changes fastest.
Arguments:
- abundance: bfloat16 [128, 32768], P('sample', 'branch'), may hold values from 0.01 to 100, as said below
- length_table: float32 [32768], P('branch'), may hold values from 0.01 to 1, as said below
- branch_rows: int32 [32768], P('branch'), may hold values from 0 to 16383, as said below
Outputs:
- distance: float32 [128, 128], P('sample', 'branch')
Inputs may be any that keep to these rules, and one draw needn't show every extreme that they name: `abundance`: entries are positive. `length_table`: positive branch lengths. `branch_rows`: within each aligned block of 16384 entries every number from 0 to 16383 appears once.
All inputs are finite; a program needn't handle non-finite values.
Results may differ from a plain program's by a relative error of at most 0.0003.
Values may be sent and summed in bfloat16 or wider, within the bound.
A program may use at most 64 MiB of HBM per device.

v0:
```python
import jax
import jax.numpy as jnp
from jax import lax
from jax.sharding import PartitionSpec as P


def pair_sums(mine, other, lengths):
    count, width = mine.shape
    others = other.shape[0]
    block_size = width
    while block_size > 512 and block_size % 2 == 0 and (block_size * count * others > 2097152):
        block_size = block_size // 2
    block_count = width // block_size

    def absorb(carry, turn):
        begin = turn * block_size
        left = lax.dynamic_slice_in_dim(mine, begin, block_size, 1).astype(jnp.float32)[:, None, :]
        right = lax.dynamic_slice_in_dim(other, begin, block_size, 1).astype(jnp.float32)[
            None, :, :
        ]
        weight = lax.dynamic_slice_in_dim(lengths, begin, block_size, 0)[None, None, :]
        summed = left + right
        inverse = lax.rsqrt(summed)
        return (
            (
                carry[0] + jnp.sum(weight * jnp.abs(left - right) * inverse, axis=2),
                carry[1] + jnp.sum(weight * summed * inverse, axis=2),
            ),
            None,
        )

    empty = jnp.zeros((count, others), jnp.float32)
    result, unused = lax.scan(absorb, (empty, empty), jnp.arange(block_count, dtype=jnp.int32))
    return result


def body(abundance, length_table, branch_rows):
    values = abundance.astype(jnp.float32)
    totals = lax.psum(jnp.sum(values, axis=1), "branch")
    shares = (values / totals[:, None]).astype(jnp.bfloat16)
    lengths = jnp.take(length_table, branch_rows)
    numer_part, denom_part = pair_sums(
        shares, lax.all_gather(shares, "sample", axis=0, tiled=True), lengths
    )
    summed = (
        lax.psum_scatter(numer_part, "branch", scatter_dimension=1, tiled=True),
        lax.psum_scatter(denom_part, "branch", scatter_dimension=1, tiled=True),
    )
    return summed[0] / summed[1]


def solution(mesh):
    placed = (P("sample", "branch"), P("branch"), P("branch"))
    return jax.shard_map(
        body, mesh=mesh, in_specs=placed, out_specs=P("sample", "branch"), check_vma=False
    )
```

profile of v0, /device:TPU:0, one launch (start us, length us, event | category | flops | bytes accessed | tf_op | source)
XLA Modules:
  0.0 189.8 jit_solution(10400921056080740025)
XLA Ops:
  6.5 1.2 convert_reduce_fusion
  7.8 5.9 %psum.7 = f32[8]{0:T(128)S(1)} all-reduce(f32[8]{0:T(128)S(1)} %convert_reduce_fusion), channel_id=1, replica_groups=mesh['branch'=2,'sample'=16] {'branch'}, use_global_device_ids=true, to_apply=%region_1.0 | all-reduce | flops 8 | bytes 64 | tf_op jit(solution)/shard_map/psum | solution.py:39
  13.6 1.8 fusion.4
  15.5 0.9 fusion.5
  16.4 90.5 %gather_fusion = f32[16384]{0:T(1024)S(1)} fusion(f32[16384]{0:T(1024)S(1)} %copy-done, s32[16384]{0:T(1024)S(1)} %fusion.5), kind=kCustom, calls=%fused_computation | custom fusion | bytes 196608 | tf_op jit(solution)/shard_map/jit(_take)/gather | solution.py:41
  107.0 49.9 %while.13 = (s32[]{:T(128)}, f32[8,128]{1,0:T(8,128)S(1)}, f32[8,128]{1,0:T(8,128)S(1)}, s32[8]{0:T(128)S(1)}, f32[16384]{0:T(1024)S(1)}, /*index=5*/bf16[8,1638...) while((s32[]{:T(128)}, f32[8,128]{1,0:T(8,128)S(1)}, ...), condition=%wide.region_5.6_spmd.clone, body=%wide.region_2.5_spmd.clone.sunk | while | flops 19154948 | bytes 2842813 | solution.py:33
  108.2 1.1 dynamic-slice_convert_fusion.4
  110.1 3.1 %fusion.7 = (f32[8,128]{1,0:T(8,128)S(1)}, f32[8,128]{1,0:T(8,128)S(1)}) fusion(f32[128,2048]{1,0:T(8,128)S(1)} %dynamic-slice_convert_fusion.4, f32[8,2048]{1,0:T(8,128)S(1)} %dynamic-slice_convert_fusion.5, f32[2048]{0:T(1024)S(1)} %dynamic_slice.26), kind=kLoop, calls=%fused_computation.6.clone.1 | loop fusion | flops 18872320 | bytes 1130496 | tf_op jit(solution)/shard_map/while/body/eval_jaxpr/reduce_sum | solution.py:27
  114.4 1.1 dynamic-slice_convert_fusion.4
  116.3 3.1 %fusion.7 = (f32[8,128]{1,0:T(8,128)S(1)}, f32[8,128]{1,0:T(8,128)S(1)}) fusion(f32[128,2048]{1,0:T(8,128)S(1)} %dynamic-slice_convert_fusion.4, f32[8,2048]{1,0:T(8,128)S(1)} %dynamic-slice_convert_fusion.5, f32[2048]{0:T(1024)S(1)} %dynamic_slice.26), kind=kLoop, calls=%fused_computation.6.clone.1 | loop fusion | flops 18872320 | bytes 1130496 | tf_op jit(solution)/shard_map/while/body/eval_jaxpr/reduce_sum | solution.py:27
  120.6 1.1 dynamic-slice_convert_fusion.4
  122.6 3.1 %fusion.7 = (f32[8,128]{1,0:T(8,128)S(1)}, f32[8,128]{1,0:T(8,128)S(1)}) fusion(f32[128,2048]{1,0:T(8,128)S(1)} %dynamic-slice_convert_fusion.4, f32[8,2048]{1,0:T(8,128)S(1)} %dynamic-slice_convert_fusion.5, f32[2048]{0:T(1024)S(1)} %dynamic_slice.26), kind=kLoop, calls=%fused_computation.6.clone.1 | loop fusion | flops 18872320 | bytes 1130496 | tf_op jit(solution)/shard_map/while/body/eval_jaxpr/reduce_sum | solution.py:27
  126.9 1.1 dynamic-slice_convert_fusion.4
  128.8 3.1 %fusion.7 = (f32[8,128]{1,0:T(8,128)S(1)}, f32[8,128]{1,0:T(8,128)S(1)}) fusion(f32[128,2048]{1,0:T(8,128)S(1)} %dynamic-slice_convert_fusion.4, f32[8,2048]{1,0:T(8,128)S(1)} %dynamic-slice_convert_fusion.5, f32[2048]{0:T(1024)S(1)} %dynamic_slice.26), kind=kLoop, calls=%fused_computation.6.clone.1 | loop fusion | flops 18872320 | bytes 1130496 | tf_op jit(solution)/shard_map/while/body/eval_jaxpr/reduce_sum | solution.py:27
  133.1 1.1 dynamic-slice_convert_fusion.4
  135.0 3.1 %fusion.7 = (f32[8,128]{1,0:T(8,128)S(1)}, f32[8,128]{1,0:T(8,128)S(1)}) fusion(f32[128,2048]{1,0:T(8,128)S(1)} %dynamic-slice_convert_fusion.4, f32[8,2048]{1,0:T(8,128)S(1)} %dynamic-slice_convert_fusion.5, f32[2048]{0:T(1024)S(1)} %dynamic_slice.26), kind=kLoop, calls=%fused_computation.6.clone.1 | loop fusion | flops 18872320 | bytes 1130496 | tf_op jit(solution)/shard_map/while/body/eval_jaxpr/reduce_sum | solution.py:27
  139.3 1.1 dynamic-slice_convert_fusion.4
  141.3 3.1 %fusion.7 = (f32[8,128]{1,0:T(8,128)S(1)}, f32[8,128]{1,0:T(8,128)S(1)}) fusion(f32[128,2048]{1,0:T(8,128)S(1)} %dynamic-slice_convert_fusion.4, f32[8,2048]{1,0:T(8,128)S(1)} %dynamic-slice_convert_fusion.5, f32[2048]{0:T(1024)S(1)} %dynamic_slice.26), kind=kLoop, calls=%fused_computation.6.clone.1 | loop fusion | flops 18872320 | bytes 1130496 | tf_op jit(solution)/shard_map/while/body/eval_jaxpr/reduce_sum | solution.py:27
  145.6 1.1 dynamic-slice_convert_fusion.4
  147.5 3.1 %fusion.7 = (f32[8,128]{1,0:T(8,128)S(1)}, f32[8,128]{1,0:T(8,128)S(1)}) fusion(f32[128,2048]{1,0:T(8,128)S(1)} %dynamic-slice_convert_fusion.4, f32[8,2048]{1,0:T(8,128)S(1)} %dynamic-slice_convert_fusion.5, f32[2048]{0:T(1024)S(1)} %dynamic_slice.26), kind=kLoop, calls=%fused_computation.6.clone.1 | loop fusion | flops 18872320 | bytes 1130496 | tf_op jit(solution)/shard_map/while/body/eval_jaxpr/reduce_sum | solution.py:27
  151.8 1.1 dynamic-slice_convert_fusion.4
  153.7 3.1 %fusion.7 = (f32[8,128]{1,0:T(8,128)S(1)}, f32[8,128]{1,0:T(8,128)S(1)}) fusion(f32[128,2048]{1,0:T(8,128)S(1)} %dynamic-slice_convert_fusion.4, f32[8,2048]{1,0:T(8,128)S(1)} %dynamic-slice_convert_fusion.5, f32[2048]{0:T(1024)S(1)} %dynamic_slice.26), kind=kLoop, calls=%fused_computation.6.clone.1 | loop fusion | flops 18872320 | bytes 1130496 | tf_op jit(solution)/shard_map/while/body/eval_jaxpr/reduce_sum | solution.py:27
  158.4 11.2 %reduce-scatter.7.cloned.1.call-done = f32[64,8]{1,0:T(8,128)} async-done(((f32[128,8]{1,0:T(8,128)}), f32[64,8]{1,0:T(8,128)}) %reduce-scatter.7.cloned.1.call-update) | async-done | bytes 2064
  170.4 11.4 %reduce-scatter.9.cloned.1.call-done = f32[64,8]{1,0:T(8,128)} async-done(((f32[128,8]{1,0:T(8,128)}), f32[64,8]{1,0:T(8,128)}) %reduce-scatter.9.cloned.1.call-update) | async-done | bytes 2064
  (52 shorter events, 14.8 us)
Async XLA Ops:
  6.5 9.8 %copy-start = (f32[16384]{0:T(1024)S(1)}, f32[16384]{0:T(1024)}, u32[]{:S(2)}) copy-start(f32[16384]{0:T(1024)} %param.6) | copy-start | bytes 196612
  6.5 100.4 %all-gather.2.cloned.1.call-start = ((), (), s32[]{:S(2)}) async-start(), calls=%async_computation.2 | async-start | bytes 4456448 | tf_op jit(solution)/shard_map/all_gather | solution.py:43
  15.4 154.1 %reduce-scatter.7.cloned.1.call-start = ((), (), s32[]{:S(2)}) async-start(), calls=%async_computation.3 | async-start | bytes 98304
  16.4 90.6 %copy-start.1 = (s32[16384]{0:T(1024)S(1)}, s32[16384]{0:T(1024)}, u32[]{:S(2)}) copy-start(s32[16384]{0:T(1024)} %param.7) | copy-start | bytes 196612
  157.6 24.2 %reduce-scatter.9.cloned.1.call-start = ((), (), s32[]{:S(2)}) async-start(), calls=%async_computation.4 | async-start | bytes 98304
Sparse Core Ops, SparseCore 0:
  15.5 52.1 all-gather.1
  157.7 11.7 reduce-scatter.6
  171.8 10.0 reduce-scatter.8
where the time goes:
time: 191 us; the launch traced here: 190 us
  local copies, waits for them, and re-layouts  98.4 us (52%)
  other arithmetic  44.6 us (23%)
  waiting for transfers between devices  22.7 us (12%)
  between operations  13.2 us (7%)
  blocking collectives  5.86 us (3%)
  loops' own time  5.01 us (3%)
    gather x1, local copies, waits for them, and re-layouts, body(): lengths = jnp.take(length_table, branch_rows)  90.5 us
    reduce_sum x8, other arithmetic, absorb(): jnp.sum(weight * summed * inverse, axis=2)  24.7 us
    unnamed x5, waiting for transfers between devices  22.7 us
    convert_element_type x8, other arithmetic, absorb(): lax.dynamic_slice_in_dim(other, begin, block_size, 1).astype(jnp.float32)  9.15 us
    convert_element_type x8, other arithmetic, absorb(): lax.dynamic_slice_in_dim(mine, begin, block_size, 1).astype(jnp.float32)  6.16 us
    psum x1, blocking collectives, body(): totals = lax.psum(jnp.sum(values, axis=1), 'branch')  5.86 us
    another operation x1, loops' own time, pair_sums(): lax.scan(absorb, (empty, empty), jnp.arange(block_count, dtype=jnp.int32))  5.01 us
    dynamic_slice x8, local copies, waits for them, and re-layouts, pair_sums(): lax.scan(absorb, (empty, empty), jnp.arange(block_count, dtype=jnp.int32))  4.74 us
  transfers between devices with their start and end apart: 3, of which 2 were waited for; matrix products, arithmetic and copies ran while one was open for 49% of the time, Pallas kernels for 0%

commit v1 on v0

v1 whole, which is shorter than its diff:
```python
import functools

import jax
import jax.numpy as jnp
from jax import lax
from jax.experimental import pallas as pl
from jax.experimental.pallas import tpu as pltpu
from jax.sharding import PartitionSpec as P

MESH = pl.DeviceIdType.MESH
F32 = jnp.float32
ROWS = 8
LANES = 128


def pair_sums(mine, other, lengths):
    count, width = mine.shape
    others = other.shape[0]
    block_size = width
    while block_size > 512 and block_size % 2 == 0 and (block_size * count * others > 2097152):
        block_size = block_size // 2
    block_count = width // block_size

    def absorb(carry, turn):
        begin = turn * block_size
        left = lax.dynamic_slice_in_dim(mine, begin, block_size, 1).astype(F32)[:, None, :]
        right = lax.dynamic_slice_in_dim(other, begin, block_size, 1).astype(F32)[None, :, :]
        weight = lax.dynamic_slice_in_dim(lengths, begin, block_size, 0)[None, None, :]
        summed = left + right
        inverse = lax.rsqrt(summed)
        return (
            (
                carry[0] + jnp.sum(weight * jnp.abs(left - right) * inverse, axis=2),
                carry[1] + jnp.sum(weight * summed * inverse, axis=2),
            ),
            None,
        )

    empty = jnp.zeros((count, others), F32)
    result, unused = lax.scan(absorb, (empty, empty), jnp.arange(block_count, dtype=jnp.int32))
    return result


def plain_body(abundance, length_table, branch_rows):
    values = abundance.astype(F32)
    totals = lax.psum(jnp.sum(values, axis=1), "branch")
    shares = (values / totals[:, None]).astype(jnp.bfloat16)
    lengths = jnp.take(length_table, branch_rows)
    numer_part, denom_part = pair_sums(
        shares, lax.all_gather(shares, "sample", axis=0, tiled=True), lengths
    )
    summed = (
        lax.psum_scatter(numer_part, "branch", scatter_dimension=1, tiled=True),
        lax.psum_scatter(denom_part, "branch", scatter_dimension=1, tiled=True),
    )
    return summed[0] / summed[1]


def kernel(
    axes, n_branch, n_sample, chunk,
    ab_hbm, table_hbm, rows_hbm, out_ref,
    ab, table, rows, x_buf, tot_send, tot_buf, p_ref, l2_ref, big, den, res_send, res_buf,
    local_sem, own_sem, x_send_sem, x_recv_sem, t_send_sem, t_recv_sem, r_send_sem, r_recv_sem,
):
    n_dev = n_branch * n_sample
    depth = chunk // LANES
    half = n_sample * ROWS // n_branch
    my_t = lax.axis_index("branch")
    my_s = lax.axis_index("sample")
    me = my_t * n_sample + my_s

    def place(t, s):
        where = {"branch": t, "sample": s}
        return tuple(where[name] for name in axes)

    def peer_at(k):
        flat = lax.rem(me + k, n_dev)
        return flat, flat // n_sample, lax.rem(flat, n_sample)

    ab_copy = pltpu.make_async_copy(ab_hbm, ab, local_sem.at[0])
    table_copy = pltpu.make_async_copy(table_hbm, table, local_sem.at[1])
    rows_copy = pltpu.make_async_copy(rows_hbm.at[my_s], rows, local_sem.at[2])
    own_copy = pltpu.make_async_copy(
        ab_hbm.at[:, pl.ds(pl.multiple_of(my_s * chunk, chunk), chunk)], x_buf.at[my_s], own_sem
    )
    ab_copy.start()
    table_copy.start()
    rows_copy.start()
    own_copy.start()

    barrier = pltpu.get_barrier_semaphore()

    def greet(k, carry):
        flat, t, s = peer_at(k)
        pl.semaphore_signal(barrier, inc=1, device_id=place(t, s), device_id_type=MESH)
        return carry

    lax.fori_loop(1, n_dev, greet, 0)
    pl.semaphore_wait(barrier, n_dev - 1)

    def x_copy(to_s, slot, recv):
        return pltpu.make_async_remote_copy(
            src_ref=ab_hbm.at[:, pl.ds(pl.multiple_of(to_s * chunk, chunk), chunk)],
            dst_ref=x_buf.at[slot],
            send_sem=x_send_sem.at[to_s],
            recv_sem=x_recv_sem.at[recv],
            device_id=place(my_t, to_s),
            device_id_type=MESH,
        )

    def send_x(k, carry):
        x_copy(lax.rem(my_s + k, n_sample), my_s, my_s).start()
        return carry

    lax.fori_loop(1, n_sample, send_x, 0)

    lane = lax.broadcasted_iota(jnp.int32, (ROWS, LANES), 1)
    sub = lax.broadcasted_iota(jnp.int32, (ROWS, LANES), 0)
    eye = lane == sub

    ab_copy.wait()
    step = min(chunk, 1024)

    def add_up(turn, acc):
        return acc + ab[:, pl.ds(pl.multiple_of(turn * step, step), step)].astype(F32)

    acc = lax.fori_loop(0, n_sample * chunk // step, add_up, jnp.zeros((ROWS, step), F32))
    part = jnp.sum(acc, axis=1, keepdims=True)
    line = jnp.sum(jnp.where(eye, part, 0.0), axis=0, keepdims=True)
    tot_send[...] = line
    tot_buf[me] = line

    def t_copy(flat, t, s, slot):
        return pltpu.make_async_remote_copy(
            src_ref=tot_send,
            dst_ref=tot_buf.at[slot],
            send_sem=t_send_sem.at[flat],
            recv_sem=t_recv_sem.at[slot],
            device_id=place(t, s),
            device_id_type=MESH,
        )

    def send_t(k, carry):
        flat, t, s = peer_at(k)
        t_copy(flat, t, s, me).start()
        return carry

    lax.fori_loop(1, n_dev, send_t, 0)

    table_copy.wait()
    rows_copy.wait()
    index = rows[...]
    high, low = index // LANES, index % LANES

    def look_up(h, found):
        line = jnp.broadcast_to(table[pl.ds(h, 1), :], (depth, LANES))
        picked = jnp.take_along_axis(line, low, axis=1, mode="promise_in_bounds")
        return jnp.where(high == h, picked, found)

    lengths = lax.fori_loop(
        0, table.shape[0], look_up, jnp.zeros((depth, LANES), F32), unroll=8
    )
    l2_ref[...] = lengths * lengths

    def await_t(k, carry):
        flat, t, s = peer_at(k)
        t_copy(flat, t, s, flat).wait()
        return carry

    lax.fori_loop(1, n_dev, await_t, 0)
    own_copy.wait()

    def await_x(k, carry):
        s = lax.rem(my_s + k, n_sample)
        x_copy(s, s, s).wait()
        return carry

    lax.fori_loop(1, n_sample, await_x, 0)

    def prepare(s, carry):
        total = tot_buf[s]
        for t in range(1, n_branch):
            total = total + tot_buf[t * n_sample + s]
        column = jnp.sum(
            jnp.where(eye, jnp.broadcast_to(total, (ROWS, LANES)), 0.0), axis=1, keepdims=True
        )
        for r in range(depth):
            values = x_buf[s, :, r * LANES:(r + 1) * LANES].astype(F32)
            shares = (values / column).astype(jnp.bfloat16).astype(F32)
            p_ref[s, r] = shares * l2_ref[r:r + 1, :]
        return carry

    lax.fori_loop(0, n_sample, prepare, 0)

    big[...] = jnp.zeros_like(big)
    den[...] = jnp.zeros_like(den)
    pair_count = n_sample * (n_sample + 1) // 2

    def split(turn):
        j = lax.rem(turn, n_sample)
        return lax.rem(j + turn // n_sample, n_sample), j

    def place_sums(turn, sums):
        i_block, j_block = split(turn)
        now_big, now_den = big[j_block], den[j_block]
        for i in range(ROWS):
            here = lane == i_block * ROWS + i
            now_big = jnp.where(here, jnp.sum(sums[i], axis=1, keepdims=True), now_big)
            now_den = jnp.where(here, jnp.sum(sums[ROWS + i], axis=1, keepdims=True), now_den)
        big[j_block] = now_big
        den[j_block] = now_den

    def pairs(turn):
        i_block, j_block = split(turn)
        sums = [None] * (2 * ROWS)
        for r in range(depth):
            q = p_ref[j_block, r]
            for i in range(ROWS):
                p = p_ref[i_block, r, pl.ds(i, 1), :]
                summed = p + q
                inverse = lax.rsqrt(summed)
                top = jnp.maximum(p, q) * inverse
                low_part = summed * inverse
                if r == 0:
                    sums[i], sums[ROWS + i] = top, low_part
                else:
                    sums[i] += top
                    sums[ROWS + i] += low_part
        return tuple(sums)

    def advance(turn, sums):
        place_sums(turn - 1, sums)
        return pairs(turn)

    place_sums(pair_count - 1, lax.fori_loop(1, pair_count, advance, pairs(0)))

    full = (n_sample * ROWS, LANES)
    row_block = lax.broadcasted_iota(jnp.int32, full, 0) // ROWS
    column_block = lax.broadcasted_iota(jnp.int32, full, 1) // ROWS
    apart = (column_block - row_block + n_sample) % n_sample
    mine = (2 * apart < n_sample) | ((2 * apart == n_sample) & (2 * row_block < n_sample))
    whole_big = big[...].reshape(full)
    whole_den = den[...].reshape(full)
    whole_big = jnp.where(mine, whole_big, whole_big.T)
    whole_den = jnp.where(mine, whole_den, whole_den.T)
    first = lax.broadcasted_iota(jnp.int32, full, 1) < half
    for t in range(n_branch):
        left = pltpu.roll(whole_big, (LANES - t * half) % LANES, 1) if t else whole_big
        shift = (LANES + half - t * half) % LANES
        right = pltpu.roll(whole_den, shift, 1) if shift else whole_den
        res_send[t] = jnp.where(first, left, right).reshape(n_sample, ROWS, LANES)

    def r_copy(flat, t, s, slot):
        return pltpu.make_async_remote_copy(
            src_ref=res_send.at[t, s],
            dst_ref=res_buf.at[slot],
            send_sem=r_send_sem.at[flat],
            recv_sem=r_recv_sem.at[slot],
            device_id=place(t, s),
            device_id_type=MESH,
        )

    def send_r(k, carry):
        flat, t, s = peer_at(k)
        r_copy(flat, t, s, me).start()
        return carry

    lax.fori_loop(1, n_dev, send_r, 0)
    res_buf[me] = res_send[my_t, my_s]

    def await_r(k, carry):
        flat, t, s = peer_at(k)
        r_copy(flat, t, s, flat).wait()
        return carry

    lax.fori_loop(1, n_dev, await_r, 0)
    total = res_buf[0]
    for k in range(1, n_dev):
        total = total + res_buf[k]
    out_ref[...] = total


def kernel_body(axes, n_branch, n_sample, abundance, length_table, branch_rows):
    width = abundance.shape[1]
    chunk = width // n_sample
    depth = chunk // LANES
    n_dev = n_branch * n_sample
    half = n_sample * ROWS // n_branch
    sums = pl.pallas_call(
        functools.partial(kernel, axes, n_branch, n_sample, chunk),
        out_shape=jax.ShapeDtypeStruct((ROWS, LANES), F32),
        in_specs=[pl.BlockSpec(memory_space=pl.ANY)] * 3,
        out_specs=pl.BlockSpec(memory_space=pltpu.VMEM),
        scratch_shapes=[
            pltpu.VMEM((ROWS, width), jnp.bfloat16),
            pltpu.VMEM((width // LANES, LANES), F32),
            pltpu.VMEM((depth, LANES), jnp.int32),
            pltpu.VMEM((n_sample, ROWS, chunk), jnp.bfloat16),
            pltpu.VMEM((1, LANES), F32),
            pltpu.VMEM((n_dev, 1, LANES), F32),
            pltpu.VMEM((n_sample, depth, ROWS, LANES), F32),
            pltpu.VMEM((depth, LANES), F32),
            pltpu.VMEM((n_sample, ROWS, LANES), F32),
            pltpu.VMEM((n_sample, ROWS, LANES), F32),
            pltpu.VMEM((n_branch, n_sample, ROWS, LANES), F32),
            pltpu.VMEM((n_dev, ROWS, LANES), F32),
            pltpu.SemaphoreType.DMA((3,)),
            pltpu.SemaphoreType.DMA,
            pltpu.SemaphoreType.DMA((n_sample,)),
            pltpu.SemaphoreType.DMA((n_sample,)),
            pltpu.SemaphoreType.DMA((n_dev,)),
            pltpu.SemaphoreType.DMA((n_dev,)),
            pltpu.SemaphoreType.DMA((n_dev,)),
            pltpu.SemaphoreType.DMA((n_dev,)),
        ],
        compiler_params=pltpu.CompilerParams(collective_id=0, has_side_effects=True),
    )(
        abundance,
        length_table.reshape(width // LANES, LANES),
        branch_rows.reshape(n_sample, depth, LANES),
    )
    big, den = sums[:, :half], sums[:, half:2 * half]
    return (2.0 * big - den) / den


def solution(mesh):
    n_branch, n_sample = mesh.shape["branch"], mesh.shape["sample"]
    axes = tuple(mesh.axis_names)

    def body(abundance, length_table, branch_rows):
        rows, width = abundance.shape
        fits = (
            rows == ROWS
            and n_sample * ROWS == LANES
            and n_branch > 1
            and LANES % n_branch == 0
            and width % (n_sample * ROWS * LANES) == 0
        )
        if not fits:
            return plain_body(abundance, length_table, branch_rows)
        return kernel_body(axes, n_branch, n_sample, abundance, length_table, branch_rows)

    placed = (P("sample", "branch"), P("branch"), P("branch"))
    return jax.shard_map(
        body, mesh=mesh, in_specs=placed, out_specs=P("sample", "branch"), check_vma=False
    )
```

time: 191 us -> 38.8 us (0.20)
  local copies, waits for them, and re-layouts: 98.4 us -> 0 us
  other arithmetic: 44.6 us -> 1.43 us
  Pallas kernels: 0 us -> 37.2 us
  waiting for transfers between devices: 22.7 us -> 0 us
  between operations: 13.2 us -> 0.01 us
  blocking collectives: 5.86 us -> 0 us
  loops' own time: 5.01 us -> 0 us
    gather x1 -> x0, local copies, waits for them, and re-layouts: 90.5 us -> none  [body(): lengths = jnp.take(length_table, branch_rows)]
    pallas_call x0 -> x1, Pallas kernels: none -> 37.2 us  [kernel_body(): pl.pallas_call(functools.partial(kernel, axes, n_branch, n_sample, chunk)...]
    reduce_sum x9 -> x0, other arithmetic: 26 us -> none  [the longest x8 24.7 us: absorb(): jnp.sum(weight * summed * inverse, axis=2)]
    unnamed x5 -> x0, waiting for transfers between devices: 22.7 us -> none
    convert_element_type x17 -> x0, other arithmetic: 17.1 us -> none  [the longest x8 9.15 us: absorb(): lax.dynamic_slice_in_dim(other, begin, block_size, 1).astype(jnp.float32)]
    psum x1 -> x0, blocking collectives: 5.86 us -> none  [body(): totals = lax.psum(jnp.sum(values, axis=1), 'branch')]
    another operation x1 -> x0, loops' own time: 5.01 us -> none  [pair_sums(): lax.scan(absorb, (empty, empty), jnp.arange(block_count, dtype=jnp.int32))]
    dynamic_slice x16 -> x0, local copies, waits for them, and re-layouts: 4.75 us -> none  [the longest x8 4.74 us: pair_sums(): lax.scan(absorb, (empty, empty), jnp.arange(block_count, dtype=jnp.int32))]
  transfers between devices with their start and end apart: 3 -> 0, of which waited for: 2 -> 0; matrix products, arithmetic and copies ran while one was open for 49% -> 0% of each run, Pallas kernels for 0% -> 0%
where the time goes in v1:
time: 38.8 us; the launch traced here: 38.6 us
  Pallas kernels  37.2 us (96%)
  other arithmetic  1.43 us (4%)
    pallas_call x1, Pallas kernels, kernel_body(): pl.pallas_call(functools.partial(kernel, axes, n_branch, n_sample, chunk)...  37.2 us
    div x1, other arithmetic, kernel_body(): return (2.0 * big - den) / den  1.43 us

profile of v1, /device:TPU:0, one launch (start us, length us, event | category | flops | bytes accessed | tf_op | source)
XLA Modules:
  0.0 38.6 jit_solution(12015527981546667354)
XLA Ops:
  0.0 37.2 %shard_map.37 = f32[8,128]{1,0:T(8,128)} custom-call(bf16[8,16384]{1,0:T(8,128)(2,1)} %ab_hbm.1, f32[128,128]{1,0:T(8,128)} %bitcast.2, s32[16,8,128]{2,1,0:T(8,128)} %bitcast.3), custom_call_target="tpu_custom_call" | custom-call | tf_op jit(solution)/shard_map/pallas_call | solution.py:289
  37.2 1.4 %subtract_divide_fusion = f32[8,64]{1,0:T(8,128)} fusion(f32[8,128]{1,0:T(8,128)} %shard_map.37), kind=kLoop, calls=%fused_computation | loop fusion | flops 1536 | bytes 6144 | tf_op jit(solution)/shard_map/div | solution.py:323

commit v2 on v1

--- a/solution.py
+++ b/solution.py
@@ -11,6 +11,7 @@
 F32 = jnp.float32
 ROWS = 8
 LANES = 128
+UNROLL = 5
 
 
 def pair_sums(mine, other, lengths):
@@ -74,7 +75,7 @@
         return tuple(where[name] for name in axes)
 
     def peer_at(k):
-        flat = lax.rem(me + k, n_dev)
+        flat = lax.bitwise_xor(me, k)
         return flat, flat // n_sample, lax.rem(flat, n_sample)
 
     ab_copy = pltpu.make_async_copy(ab_hbm, ab, local_sem.at[0])
@@ -96,7 +97,6 @@
         return carry
 
     lax.fori_loop(1, n_dev, greet, 0)
-    pl.semaphore_wait(barrier, n_dev - 1)
 
     def x_copy(to_s, slot, recv):
         return pltpu.make_async_remote_copy(
@@ -109,10 +109,8 @@
         )
 
     def send_x(k, carry):
-        x_copy(lax.rem(my_s + k, n_sample), my_s, my_s).start()
-        return carry
-
-    lax.fori_loop(1, n_sample, send_x, 0)
+        x_copy(lax.bitwise_xor(my_s, k), my_s, my_s).start()
+        return carry
 
     lane = lax.broadcasted_iota(jnp.int32, (ROWS, LANES), 1)
     sub = lax.broadcasted_iota(jnp.int32, (ROWS, LANES), 0)
@@ -145,7 +143,6 @@
         t_copy(flat, t, s, me).start()
         return carry
 
-    lax.fori_loop(1, n_dev, send_t, 0)
 
     table_copy.wait()
     rows_copy.wait()
@@ -162,22 +159,29 @@
     )
     l2_ref[...] = lengths * lengths
 
-    def await_t(k, carry):
-        flat, t, s = peer_at(k)
-        t_copy(flat, t, s, flat).wait()
-        return carry
-
-    lax.fori_loop(1, n_dev, await_t, 0)
-    own_copy.wait()
-
-    def await_x(k, carry):
-        s = lax.rem(my_s + k, n_sample)
-        x_copy(s, s, s).wait()
-        return carry
-
-    lax.fori_loop(1, n_sample, await_x, 0)
-
-    def prepare(s, carry):
+    pl.semaphore_wait(barrier, n_dev - 1)
+    lax.fori_loop(1, n_dev, send_t, 0)
+    lax.fori_loop(1, n_sample, send_x, 0)
+
+    near = n_sample // 2
+
+    def arrive(k, carry):
+        s = lax.bitwise_xor(my_s, k)
+        for t in range(n_branch):
+            flat = t * n_sample + s
+
+            @pl.when(flat != me)
+            def _():
+                t_copy(flat, t, s, flat).wait()
+
+        @pl.when(k > 0)
+        def _():
+            x_copy(s, s, s).wait()
+
+        return carry
+
+    def prepare(k, carry):
+        s = lax.bitwise_xor(my_s, k)
         total = tot_buf[s]
         for t in range(1, n_branch):
             total = total + tot_buf[t * n_sample + s]
@@ -190,15 +194,23 @@
             p_ref[s, r] = shares * l2_ref[r:r + 1, :]
         return carry
 
-    lax.fori_loop(0, n_sample, prepare, 0)
 
     big[...] = jnp.zeros_like(big)
     den[...] = jnp.zeros_like(den)
     pair_count = n_sample * (n_sample + 1) // 2
+    inner = near * (near + 1) // 2
 
     def split(turn):
-        j = lax.rem(turn, n_sample)
-        return lax.rem(j + turn // n_sample, n_sample), j
+        across = turn - inner
+        far = across - near * near
+        within = jnp.where(far >= 0, far, turn)
+        base = jnp.where(far >= 0, near, 0)
+        j = lax.rem(within, near)
+        i = lax.rem(j + within // near, near)
+        is_across = (across >= 0) & (far < 0)
+        i_block = jnp.where(is_across, across // near, base + i)
+        j_block = jnp.where(is_across, near + lax.rem(across, near), base + j)
+        return lax.bitwise_xor(my_s, i_block), lax.bitwise_xor(my_s, j_block)
 
     def place_sums(turn, sums):
         i_block, j_block = split(turn)
@@ -232,13 +244,22 @@
         place_sums(turn - 1, sums)
         return pairs(turn)
 
-    place_sums(pair_count - 1, lax.fori_loop(1, pair_count, advance, pairs(0)))
+    own_copy.wait()
+    lax.fori_loop(0, near, arrive, 0)
+    lax.fori_loop(0, near, prepare, 0, unroll=4)
+    sums = lax.fori_loop(1, inner, advance, pairs(0), unroll=UNROLL)
+    lax.fori_loop(near, n_sample, arrive, 0)
+    lax.fori_loop(near, n_sample, prepare, 0, unroll=4)
+    place_sums(pair_count - 1, lax.fori_loop(inner, pair_count, advance, sums, unroll=UNROLL))
 
     full = (n_sample * ROWS, LANES)
-    row_block = lax.broadcasted_iota(jnp.int32, full, 0) // ROWS
-    column_block = lax.broadcasted_iota(jnp.int32, full, 1) // ROWS
-    apart = (column_block - row_block + n_sample) % n_sample
-    mine = (2 * apart < n_sample) | ((2 * apart == n_sample) & (2 * row_block < n_sample))
+    row_block = lax.bitwise_xor(lax.broadcasted_iota(jnp.int32, full, 0) // ROWS, my_s)
+    column_block = lax.bitwise_xor(lax.broadcasted_iota(jnp.int32, full, 1) // ROWS, my_s)
+    row_at, column_at = row_block % near, column_block % near
+    apart = (column_at - row_at + near) % near
+    same = (row_block >= near) == (column_block >= near)
+    turned = (2 * apart < near) | ((2 * apart == near) & (2 * row_at < near))
+    mine = (same & turned) | ((row_block >= near) & (column_block < near))
     whole_big = big[...].reshape(full)
     whole_den = den[...].reshape(full)
     whole_big = jnp.where(mine, whole_big, whole_big.T)

time: 38.8 us -> 32.2 us (0.83)
  Pallas kernels: 37.2 us -> 30.6 us
    pallas_call x1, Pallas kernels: 37.2 us -> 30.6 us  [kernel_body(): pl.pallas_call(functools.partial(kernel, axes, n_branch, n_sample, chunk)...]
where the time goes in v2:
time: 32.2 us; the launch traced here: 32 us
  Pallas kernels  30.6 us (95%)
  other arithmetic  1.43 us (4%)
    pallas_call x1, Pallas kernels, kernel_body(): pl.pallas_call(functools.partial(kernel, axes, n_branch, n_sample, chunk)...  30.6 us
    div x1, other arithmetic, kernel_body(): return (2.0 * big - den) / den  1.43 us

profile of v2, /device:TPU:0, one launch (start us, length us, event | category | flops | bytes accessed | tf_op | source)
XLA Modules:
  0.0 32.0 jit_solution(14798986104381143027)
XLA Ops:
  0.0 30.6 %shard_map.37 = f32[8,128]{1,0:T(8,128)} custom-call(bf16[8,16384]{1,0:T(8,128)(2,1)} %ab_hbm.1, f32[128,128]{1,0:T(8,128)} %bitcast.2, s32[16,8,128]{2,1,0:T(8,128)} %bitcast.3), custom_call_target="tpu_custom_call" | custom-call | tf_op jit(solution)/shard_map/pallas_call | solution.py:310
  30.6 1.4 %subtract_divide_fusion = f32[8,64]{1,0:T(8,128)} fusion(f32[8,128]{1,0:T(8,128)} %shard_map.37), kind=kLoop, calls=%fused_computation | loop fusion | flops 1536 | bytes 6144 | tf_op jit(solution)/shard_map/div | solution.py:344

commit v3 on v2

--- a/solution.py
+++ b/solution.py
@@ -11,7 +11,8 @@
 F32 = jnp.float32
 ROWS = 8
 LANES = 128
-UNROLL = 5
+UNROLL = 16
+STAGES = 4
 
 
 def pair_sums(mine, other, lengths):
@@ -163,7 +164,7 @@
     lax.fori_loop(1, n_dev, send_t, 0)
     lax.fori_loop(1, n_sample, send_x, 0)
 
-    near = n_sample // 2
+    group = n_sample // STAGES
 
     def arrive(k, carry):
         s = lax.bitwise_xor(my_s, k)
@@ -197,23 +198,19 @@
 
     big[...] = jnp.zeros_like(big)
     den[...] = jnp.zeros_like(den)
-    pair_count = n_sample * (n_sample + 1) // 2
-    inner = near * (near + 1) // 2
-
-    def split(turn):
-        across = turn - inner
-        far = across - near * near
-        within = jnp.where(far >= 0, far, turn)
-        base = jnp.where(far >= 0, near, 0)
-        j = lax.rem(within, near)
-        i = lax.rem(j + within // near, near)
-        is_across = (across >= 0) & (far < 0)
-        i_block = jnp.where(is_across, across // near, base + i)
-        j_block = jnp.where(is_across, near + lax.rem(across, near), base + j)
+    within = group * (group + 1) // 2
+
+    def split(stage, turn):
+        base = stage * group
+        across = turn - within
+        j = lax.rem(turn, group)
+        i = lax.rem(j + turn // group, group)
+        i_block = jnp.where(across >= 0, across // group, base + i)
+        j_block = base + jnp.where(across >= 0, lax.rem(across, group), j)
         return lax.bitwise_xor(my_s, i_block), lax.bitwise_xor(my_s, j_block)
 
-    def place_sums(turn, sums):
-        i_block, j_block = split(turn)
+    def place_sums(stage, turn, sums):
+        i_block, j_block = split(stage, jnp.int32(turn))
         now_big, now_den = big[j_block], den[j_block]
         for i in range(ROWS):
             here = lane == i_block * ROWS + i
@@ -222,44 +219,56 @@
         big[j_block] = now_big
         den[j_block] = now_den
 
-    def pairs(turn):
-        i_block, j_block = split(turn)
-        sums = [None] * (2 * ROWS)
-        for r in range(depth):
-            q = p_ref[j_block, r]
-            for i in range(ROWS):
+    def pairs(stage, turn):
+        i_block, j_block = split(stage, jnp.int32(turn))
+        tops, lows = [], []
+        others = [p_ref[j_block, r] for r in range(depth)]
+        for i in range(ROWS):
+            top = low_part = None
+            for r in range(depth):
                 p = p_ref[i_block, r, pl.ds(i, 1), :]
+                q = others[r]
                 summed = p + q
                 inverse = lax.rsqrt(summed)
-                top = jnp.maximum(p, q) * inverse
-                low_part = summed * inverse
-                if r == 0:
-                    sums[i], sums[ROWS + i] = top, low_part
-                else:
-                    sums[i] += top
-                    sums[ROWS + i] += low_part
-        return tuple(sums)
-
-    def advance(turn, sums):
-        place_sums(turn - 1, sums)
-        return pairs(turn)
+                more_top = jnp.maximum(p, q) * inverse
+                more_low = summed * inverse
+                top = more_top if r == 0 else top + more_top
+                low_part = more_low if r == 0 else low_part + more_low
+            tops.append(top)
+            lows.append(low_part)
+        return tuple(tops + lows)
 
     own_copy.wait()
-    lax.fori_loop(0, near, arrive, 0)
-    lax.fori_loop(0, near, prepare, 0, unroll=4)
-    sums = lax.fori_loop(1, inner, advance, pairs(0), unroll=UNROLL)
-    lax.fori_loop(near, n_sample, arrive, 0)
-    lax.fori_loop(near, n_sample, prepare, 0, unroll=4)
-    place_sums(pair_count - 1, lax.fori_loop(inner, pair_count, advance, sums, unroll=UNROLL))
+    sums, before = None, None
+    for stage in range(STAGES):
+        count = within + stage * group * group
+        head = count % UNROLL or UNROLL
+        lax.fori_loop(stage * group, (stage + 1) * group, arrive, 0)
+        lax.fori_loop(stage * group, (stage + 1) * group, prepare, 0, unroll=group)
+        for turn in range(head):
+            if before is not None:
+                place_sums(*before, sums)
+            sums, before = pairs(stage, turn), (stage, turn)
+
+        def advance(loop, sums, stage=stage, head=head):
+            for u in range(UNROLL):
+                turn = head + loop * UNROLL + u
+                place_sums(stage, turn - 1, sums)
+                sums = pairs(stage, turn)
+            return sums
+
+        sums = lax.fori_loop(0, (count - head) // UNROLL, advance, sums)
+        before = (stage, count - 1)
+    place_sums(*before, sums)
 
     full = (n_sample * ROWS, LANES)
     row_block = lax.bitwise_xor(lax.broadcasted_iota(jnp.int32, full, 0) // ROWS, my_s)
     column_block = lax.bitwise_xor(lax.broadcasted_iota(jnp.int32, full, 1) // ROWS, my_s)
-    row_at, column_at = row_block % near, column_block % near
-    apart = (column_at - row_at + near) % near
-    same = (row_block >= near) == (column_block >= near)
-    turned = (2 * apart < near) | ((2 * apart == near) & (2 * row_at < near))
-    mine = (same & turned) | ((row_block >= near) & (column_block < near))
+    row_at, column_at = row_block % group, column_block % group
+    row_stage, column_stage = row_block // group, column_block // group
+    apart = (column_at - row_at + group) % group
+    turned = (2 * apart < group) | ((2 * apart == group) & (2 * row_at < group))
+    mine = ((row_stage == column_stage) & turned) | (row_stage > column_stage)
     whole_big = big[...].reshape(full)
     whole_den = den[...].reshape(full)
     whole_big = jnp.where(mine, whole_big, whole_big.T)
@@ -309,7 +318,7 @@
     half = n_sample * ROWS // n_branch
     sums = pl.pallas_call(
         functools.partial(kernel, axes, n_branch, n_sample, chunk),
-        out_shape=jax.ShapeDtypeStruct((ROWS, LANES), F32),
+        out_shape=pltpu.VMEM((ROWS, LANES), F32),
         in_specs=[pl.BlockSpec(memory_space=pl.ANY)] * 3,
         out_specs=pl.BlockSpec(memory_space=pltpu.VMEM),
         scratch_shapes=[
@@ -355,6 +364,7 @@
             and n_sample * ROWS == LANES
             and n_branch > 1
             and LANES % n_branch == 0
+            and n_sample % STAGES == 0
             and width % (n_sample * ROWS * LANES) == 0
         )
         if not fits:

time: 32.2 us -> 28.9 us (0.90)
  Pallas kernels: 30.6 us -> 28 us
  other arithmetic: 1.43 us -> 0.67 us
    pallas_call x1, Pallas kernels: 30.6 us -> 28 us  [kernel_body(): pl.pallas_call(functools.partial(kernel, axes, n_branch, n_sample, chunk)...]
    div x1, other arithmetic: 1.43 us -> 0.67 us  [kernel_body(): return (2.0 * big - den) / den]
where the time goes in v3:
time: 28.9 us; the launch traced here: 28.7 us
  Pallas kernels  28 us (97%)
  other arithmetic  0.67 us (2%)
    pallas_call x1, Pallas kernels, kernel_body(): pl.pallas_call(functools.partial(kernel, axes, n_branch, n_sample, chunk)...  28 us
    div x1, other arithmetic, kernel_body(): return (2.0 * big - den) / den  0.67 us

profile of v3, /device:TPU:0, one launch (start us, length us, event | category | flops | bytes accessed | tf_op | source)
XLA Modules:
  0.0 28.7 jit_solution(13713984000128686614)
XLA Ops:
  0.0 28.0 %shard_map.37 = f32[8,128]{1,0:T(8,128)S(1)} custom-call(bf16[8,16384]{1,0:T(8,128)(2,1)} %ab_hbm.1, f32[128,128]{1,0:T(8,128)} %bitcast.2, s32[16,8,128]{2,1,0:T(8,128)} %bitcast.3), custom_call_target="tpu_custom_call" | custom-call | tf_op jit(solution)/shard_map/pallas_call | solution.py:319
  28.1 0.7 %subtract_divide_fusion = f32[8,64]{1,0:T(8,128)} fusion(f32[8,128]{1,0:T(8,128)S(1)} %shard_map.37), kind=kLoop, calls=%fused_computation | loop fusion | flops 1536 | bytes 6144 | tf_op jit(solution)/shard_map/div | solution.py:353
